TPU v7x, 512 devices: a whole 4x4x16 slice. The times are simulated.
512 devices in a mesh: seq: 64 (over z_lo, y, core), dp: 8 (over z_hi, x).
Axes of the slice: x: 4, y: 4, z: 16 (z_hi: 2, z_lo: 8; z = z_hi * 8 + z_lo), core: 2. Of those that a mesh axis runs over, the one named last changes fastest.
Arguments:
- q_raw: bfloat16 [8, 16384, 1024], P('dp', 'seq'), may hold values from -400 to 400
- k_raw: bfloat16 [8, 16384, 512], P('dp', 'seq'), may hold values from -400 to 400
- values: bfloat16 [8, 16384, 512], P('dp', 'seq'), may hold values from -6 to 6
- grad_out: bfloat16 [8, 16384, 1024], P('dp', 'seq'), may hold values from -80 to 80
- q_gain: float32 [256], replicated, may hold values from 0.5 to 7
- k_gain: float32 [256], replicated, may hold values from 0.5 to 7
Outputs:
- grad_q_raw: bfloat16 [8, 16384, 1024], P('dp', 'seq')
- grad_k_raw: bfloat16 [8, 16384, 512], P('dp', 'seq')
- grad_values: bfloat16 [8, 16384, 512], P('dp', 'seq')
- grad_q_gain: float32 [256], replicated
- grad_k_gain: float32 [256], replicated
All inputs are finite; a program needn't handle non-finite values.
Results may differ from a plain program's by a relative error of at most 0.029.
The roundings to bfloat16 on the way count: a program that leaves them out, or rounds other values in their place, can miss the bound.
Values may be sent and summed in bfloat16 or wider, within the bound.
A program may use at most 128 MiB of HBM per device.

v0:
```python
import jax
import jax.numpy as jnp
from jax import lax
from jax.sharding import PartitionSpec as P

WINDOW = 1024
EPS = 1e-06
ROPE_BASE = 10000.0
MASKED = -1e30


def from_behind(array, axis, by):
    count = lax.axis_size(axis)
    pairs = [(i, i + by) for i in range(count) if 0 <= i + by < count]
    return lax.ppermute(array, axis, pairs)


def rope_tables(positions, head_size):
    half_size = head_size // 2
    freqs = jnp.power(ROPE_BASE, -(2.0 * jnp.arange(half_size, dtype=jnp.float32)) / head_size)
    angles = positions.astype(jnp.float32)[:, None] * freqs[None, :]
    return (jnp.cos(angles), jnp.sin(angles))


def norm_rope(raw_in, gain_in, cosine, sine, head_count):
    head_size = gain_in.shape[0]
    row_count = raw_in.shape[0]
    inputs = raw_in.reshape(row_count, head_count, head_size)
    inverse = lax.rsqrt(jnp.mean(inputs * inputs, axis=-1, keepdims=True) + EPS)
    scaled = inputs * inverse * gain_in
    half_size = head_size // 2
    lower = scaled[..., :half_size]
    upper = scaled[..., half_size:]
    cos_rows = cosine[:, None, :]
    sin_rows = sine[:, None, :]
    turned = jnp.concatenate(
        [lower * cos_rows - upper * sin_rows, upper * cos_rows + lower * sin_rows], axis=-1
    )
    return turned.reshape(row_count, head_count * head_size)


def local(q_raw, k_raw, values, grad_out, q_gain, k_gain):
    q_local = q_raw[0]
    k_local = k_raw[0]
    v_local = values[0]
    do_local = grad_out[0]
    rows_here = q_local.shape[0]
    head_size = q_gain.shape[0]
    query_heads = q_local.shape[1] // head_size
    pair_heads = k_local.shape[1] // head_size
    group_size = query_heads // pair_heads
    reach_dev = WINDOW // rows_here
    key_span = WINDOW + rows_here
    score_scale = head_size ** (-0.5)
    first_pos = lax.axis_index("seq") * rows_here
    positions = first_pos + jnp.arange(rows_here, dtype=jnp.int32)
    cosine, sine = rope_tables(positions, head_size)
    q_rot32, q_back = jax.vjp(
        lambda raw_in, gain_in: norm_rope(raw_in, gain_in, cosine, sine, query_heads),
        q_local.astype(jnp.float32),
        q_gain,
    )
    k_rot32, k_back = jax.vjp(
        lambda raw_in, gain_in: norm_rope(raw_in, gain_in, cosine, sine, pair_heads),
        k_local.astype(jnp.float32),
        k_gain,
    )
    q_rot = q_rot32.astype(jnp.bfloat16)
    k_rot = k_rot32.astype(jnp.bfloat16)
    halo_k = []
    halo_v = []
    for offset in range(reach_dev, 0, -1):
        received = from_behind((k_rot, v_local), "seq", offset)
        halo_k.append(received[0])
        halo_v.append(received[1])
    key_rows = jnp.concatenate(halo_k + [k_rot], axis=0)
    value_rows = jnp.concatenate(halo_v + [v_local], axis=0)
    q_heads = q_rot.reshape(rows_here, pair_heads, group_size, head_size)
    k_heads = key_rows.reshape(key_span, pair_heads, head_size)
    v_heads = value_rows.reshape(key_span, pair_heads, head_size)
    do_heads = do_local.reshape(rows_here, pair_heads, group_size, head_size)
    query_idx = jnp.arange(rows_here, dtype=jnp.int32)[:, None]
    key_idx = jnp.arange(key_span, dtype=jnp.int32)[None, :]
    distance = query_idx + WINDOW - key_idx
    visible = (distance >= 0) & (distance < WINDOW) & (key_idx >= WINDOW - first_pos)
    scores = (
        jnp.einsum("tkgd,skd->kgts", q_heads, k_heads, preferred_element_type=jnp.float32)
        * score_scale
    )
    scores = jnp.where(visible, scores, MASKED)
    row_top = jnp.max(scores, axis=-1, keepdims=True)
    row_total = jnp.log(jnp.sum(jnp.exp(scores - row_top), axis=-1, keepdims=True)) + row_top
    weights = jnp.exp(scores - row_total)
    weights_b = weights.astype(jnp.bfloat16)
    dweights = jnp.einsum("tkgd,skd->kgts", do_heads, v_heads, preferred_element_type=jnp.float32)
    row_delta = jnp.sum(weights * dweights, axis=-1, keepdims=True)
    dscores = (weights * (dweights - row_delta) * score_scale).astype(jnp.bfloat16)
    dq_rot = jnp.einsum(
        "kgts,skd->tkgd", dscores, k_heads, preferred_element_type=jnp.float32
    ).reshape(rows_here, query_heads * head_size)
    dk_all = jnp.einsum("kgts,tkgd->skd", dscores, q_heads, preferred_element_type=jnp.float32)
    dv_all = jnp.einsum("kgts,tkgd->skd", weights_b, do_heads, preferred_element_type=jnp.float32)
    dk_own = dk_all[WINDOW:]
    dv_own = dv_all[WINDOW:]
    for offset in range(1, reach_dev + 1):
        low_row = (reach_dev - offset) * rows_here
        sent_k = dk_all[low_row : low_row + rows_here].astype(jnp.bfloat16)
        sent_v = dv_all[low_row : low_row + rows_here].astype(jnp.bfloat16)
        received = from_behind((sent_k, sent_v), "seq", -offset)
        dk_own = dk_own + received[0].astype(jnp.float32)
        dv_own = dv_own + received[1].astype(jnp.float32)
    dk_rot = dk_own.reshape(rows_here, pair_heads * head_size)
    grad_q_local, gain_q_local = q_back(dq_rot)
    grad_k_local, gain_k_local = k_back(dk_rot)
    gain_q_all, gain_k_all = lax.psum((gain_q_local, gain_k_local), ("seq", "dp"))
    grad_v_local = dv_own.reshape(rows_here, pair_heads * head_size).astype(jnp.bfloat16)
    return (
        grad_q_local.astype(jnp.bfloat16)[None],
        grad_k_local.astype(jnp.bfloat16)[None],
        grad_v_local[None],
        gain_q_all,
        gain_k_all,
    )


def solution(mesh):
    return jax.shard_map(
        local,
        mesh=mesh,
        in_specs=(
            P("dp", "seq", None),
            P("dp", "seq", None),
            P("dp", "seq", None),
            P("dp", "seq", None),
            P(),
            P(),
        ),
        out_specs=(P("dp", "seq", None), P("dp", "seq", None), P("dp", "seq", None), P(), P()),
        check_vma=False,
    )
```

profile of v0, /device:TPU:1, one launch (start us, length us, event | category | flops | bytes accessed | tf_op | source)
XLA Modules:
  0.0 258.1 jit_solution(8285778720912913618)
XLA Ops:
  0.7 1.1 copy.101
  1.9 0.8 multiply_multiply_fusion.1
  2.7 0.5 multiply_cosine_fusion
  3.4 6.4 %collective-permute-start = (bf16[256,512]{0,1:T(8,128)(2,1)S(1)}, bf16[256,512]{0,1:T(8,128)(2,1)}, u32[]{:S(2)}, u32[]{:S(2)}) collective-permute-start(bf16[256,512]{0,1:T(8,128)(2,1)S(1)} %bitcast.80), channel_id=1, source_target_pairs={{0,32},{8,40},{16,48},{24,56},{32,64},{40,72},{48,80},{56,88},{64,... | collective-permute-start | bytes 786440 | tf_op jit(solution)/shard_map/ppermute | solution.py:15
  9.7 4.2 %collective-permute-start.1 = (bf16[256,512]{0,1:T(8,128)(2,1)S(1)}, bf16[256,512]{0,1:T(8,128)(2,1)}, u32[]{:S(2)}, u32[]{:S(2)}) collective-permute-start(bf16[256,512]{0,1:T(8,128)(2,1)S(1)} %bitcast.81), channel_id=1, source_target_pairs={{0,24},{8,32},{16,40},{24,48},{32,56},{40,64},{48,72},{56,80},{64,... | collective-permute-start | bytes 786440 | tf_op jit(solution)/shard_map/ppermute | solution.py:15
  13.9 3.2 %collective-permute-start.2 = (bf16[256,512]{0,1:T(8,128)(2,1)S(1)}, bf16[256,512]{0,1:T(8,128)(2,1)}, u32[]{:S(2)}, u32[]{:S(2)}) collective-permute-start(bf16[256,512]{0,1:T(8,128)(2,1)S(1)} %bitcast.82), channel_id=1, source_target_pairs={{0,16},{8,24},{16,32},{24,40},{32,48},{40,56},{48,64},{56,72},{64,... | collective-permute-start | bytes 786440 | tf_op jit(solution)/shard_map/ppermute | solution.py:15
  17.1 1.9 collective-permute-start.3
  19.2 4.7 %collective-permute-start.4 = (bf16[256,512]{0,1:T(8,128)(2,1)S(1)}, bf16[256,512]{0,1:T(8,128)(2,1)}, u32[]{:S(2)}, u32[]{:S(2)}) collective-permute-start(bf16[256,512]{0,1:T(8,128)(2,1)S(1)} %bitcast.85), channel_id=1, source_target_pairs={{0,32},{8,40},{16,48},{24,56},{32,64},{40,72},{48,80},{56,88},{64,... | collective-permute-start | bytes 786440 | tf_op jit(solution)/shard_map/ppermute | solution.py:15
  24.1 0.5 reshape.191
  24.6 0.3 multiply_reduce_fusion.2
  25.2 0.3 multiply_multiply_fusion
  25.6 1.1 fusion.20
  26.7 0.3 subtract_convert_fusion
  27.0 0.3 pad_maximum_fusion
  27.3 1.2 copy.142
  28.5 0.8 copy.114
  29.4 0.9 copy.106
  30.3 3.4 %collective-permute-start.5 = (bf16[256,512]{0,1:T(8,128)(2,1)S(1)}, bf16[256,512]{0,1:T(8,128)(2,1)S(1)}, u32[]{:S(2)}, u32[]{:S(2)}) collective-permute-start(bf16[256,512]{0,1:T(8,128)(2,1)S(1)} %bitcast.87), channel_id=1, source_target_pairs={{0,24},{8,32},{16,40},{24,48},{32,56},{40,64},{48,72},{56,80},{64,... | collective-permute-start | bytes 786440 | tf_op jit(solution)/shard_map/ppermute | solution.py:15
  33.7 1.0 constant_dynamic-update-slice_fusion.4
  34.6 3.9 %collective-permute-start.6 = (bf16[256,512]{0,1:T(8,128)(2,1)S(1)}, bf16[256,512]{0,1:T(8,128)(2,1)}, u32[]{:S(2)}, u32[]{:S(2)}) collective-permute-start(bf16[256,512]{0,1:T(8,128)(2,1)S(1)} %bitcast.88), channel_id=1, source_target_pairs={{0,16},{8,24},{16,32},{24,40},{32,48},{40,56},{48,64},{56,72},{64,... | collective-permute-start | bytes 786440 | tf_op jit(solution)/shard_map/ppermute | solution.py:15
  38.5 1.0 constant_dynamic-update-slice_fusion.3
  39.5 2.2 collective-permute-start.7
  41.7 1.0 constant_dynamic-update-slice_fusion.2
  42.7 1.0 constant_dynamic-update-slice_fusion.1
  43.7 1.0 copy-done.11
  44.7 1.1 copy.110
  45.8 0.7 copy-done.10
  46.5 1.1 copy.111
  47.6 1.8 copy.112
  49.4 0.7 constant_dynamic-update-slice_fusion
  50.1 0.7 constant_dynamic-update-slice_fusion.9
  50.9 1.1 copy.113
  52.0 3.0 %fusion.39 = (f32[2,2,256]{2,1,0:T(2,128)S(1)}, f32[2,2,256,1280]{2,3,1,0:T(8,128)S(1)}) fusion(bf16[1280,2,256,1]{0,2,3,1:T(8,128)(2,1)} %bitcast.94, bf16[256,2,2,256]{3,0,2,1:T(8,128)(2,1)} %bitcast.91, pred[256,1280]{0,1:T(8,128)(4,1)} %fusion.20), kind=kOutput, calls=%fused_computation.89 | convolution fusion | flops 675019776 | bytes 7409664 | tf_op jit(solution)/shard_map/tkgd,skd->kgts/dot_general | solution.py:87
  55.0 0.7 exponential_reduce_fusion
  55.7 1.7 copy-done
  57.8 3.2 %fusion.15 = f32[2,1280,256,2]{2,1,3,0:T(8,128)} fusion(bf16[256,2,2,256]{0,3,2,1:T(8,128)(2,1)S(1)} %bitcast.76, bf16[1280,2,256]{2,0,1:T(8,128)(2,1)S(1)} %constant_dynamic-update-slice_fusion.5), kind=kOutput, calls=%fused_computation.20 | convolution fusion | flops 671088640 | bytes 7077888 | tf_op jit(solution)/shard_map/tkgd,skd->kgts/dot_general | solution.py:95
  61.0 10.9 %fusion.6 = f32[2,256,2,256]{3,1,2,0:T(8,128)} fusion(bf16[1280,2,256,1]{0,2,3,1:T(8,128)(2,1)} %bitcast.95, f32[2,1280,256,2]{2,1,3,0:T(8,128)} %fusion.15, f32[2,2,256,1280]{2,3,1,0:T(8,128)} %copy-done, f32[2,2,256]{2,1,0:T(2,128)S(1)} %log_add_fusion), kind=kOutput, calls=%fused_computation.13 | convolution fusion | flops 680265984 | bytes 12849152 | tf_op jit(solution)/shard_map/kgts,skd->tkgd/dot_general | solution.py:98
  71.8 11.7 %fusion.40 = (bf16[1280,2,256]{0,2,1:T(8,128)(2,1)}, f32[1280,2,256]{0,2,1:T(8,128)}) fusion(bf16[256,2,2,256]{3,0,2,1:T(8,128)(2,1)S(1)} %bitcast.92, f32[2,1280,256,2]{2,1,3,0:T(8,128)} %fusion.15, f32[2,2,256,1280]{2,3,1,0:T(8,128)} %copy-done, f32[2,2,256]{2,1,0:T(2,128)S(1)} %log_add_fusion), kind=kOutput, calls=%fused_computation.90 | convolution fusion | flops 680921344 | bytes 14946304 | tf_op jit(solution)/shard_map/kgts,tkgd->skd/dot_general | solution.py:101
  83.6 5.4 %fusion.41 = (bf16[1280,2,256]{0,2,1:T(8,128)(2,1)}, f32[1280,2,256]{0,2,1:T(8,128)}) fusion(bf16[256,2,2,256]{0,3,2,1:T(8,128)(2,1)S(1)} %bitcast.77, f32[2,2,256,1280]{2,3,1,0:T(8,128)} %copy-done, f32[2,2,256]{2,1,0:T(2,128)S(1)} %log_add_fusion), kind=kOutput, calls=%fused_computation.91 | convolution fusion | flops 674365440 | bytes 9703424 | tf_op jit(solution)/shard_map/kgts,tkgd->skd/dot_general | solution.py:102
  89.3 1.0 copy.140
  90.3 1.4 multiply_add_fusion.1
  91.7 1.2 multiply_reduce_fusion
  93.0 0.8 copy.120
  93.9 2.2 fusion.37
  96.0 1.3 collective-permute-start.11
  97.3 1.3 collective-permute-start.10
  98.6 1.3 collective-permute-start.9
  99.9 3.1 %collective-permute-start.8 = (bf16[256,2,256]{0,2,1:T(8,128)(2,1)}, bf16[256,2,256]{0,2,1:T(8,128)(2,1)}, u32[]{:S(2)}, u32[]{:S(2)}) collective-permute-start(bf16[256,2,256]{0,2,1:T(8,128)(2,1)} %get-tuple-element.40), channel_id=1, source_target_pairs={{8,0},{16,8},{24,16},{32,24},{40,32},{48,40},{56,48},{64,56},{72,6... | collective-permute-start | bytes 786440 | tf_op jit(solution)/shard_map/ppermute | solution.py:15
  103.0 1.6 fusion.21
  104.6 1.2 convert_element_type.124
  105.7 2.1 fusion.36
  107.8 1.3 collective-permute-start.15
  109.1 1.3 collective-permute-start.14
  110.6 1.3 collective-permute-start.13
  111.9 10.3 %collective-permute-done.9 = bf16[256,2,256]{0,2,1:T(8,128)(2,1)} collective-permute-done((bf16[256,2,256]{0,2,1:T(8,128)(2,1)}, bf16[256,2,256]{0,2,1:T(8,128)(2,1)}, u32[]{:S(2)}, u32[]{:S(2)}) %collective-permute-start.9) | collective-permute-done | bytes 262176 | tf_op jit(solution)/shard_map/ppermute | solution.py:15
  122.1 1.9 collective-permute-start.12
  124.0 6.9 %collective-permute-done.8 = bf16[256,2,256]{0,2,1:T(8,128)(2,1)} collective-permute-done((bf16[256,2,256]{0,2,1:T(8,128)(2,1)}, bf16[256,2,256]{0,2,1:T(8,128)(2,1)}, u32[]{:S(2)}, u32[]{:S(2)}) %collective-permute-start.8) | collective-permute-done | bytes 262176 | tf_op jit(solution)/shard_map/ppermute | solution.py:15
  131.0 1.5 fusion.29
  132.9 0.8 copy.125
  133.7 6.3 %collective-permute-done.13 = bf16[256,2,256]{0,2,1:T(8,128)(2,1)S(1)} collective-permute-done((bf16[256,2,256]{0,2,1:T(8,128)(2,1)S(1)}, bf16[256,2,256]{0,2,1:T(8,128)(2,1)S(1)}, u32[]{:S(2)}, u32[]{:S(2)}) %collective-permute-start.13) | collective-permute-done | bytes 262176 | tf_op jit(solution)/shard_map/ppermute | solution.py:15
  140.0 1.9 collective-permute-done.12
  142.0 1.2 fusion.26
  143.2 0.8 copy.126
  144.0 114.1 %all-reduce.4 = (f32[256]{0:T(256)}, f32[256]{0:T(256)}) all-reduce(f32[256]{0:T(256)S(1)} %copy-done.15, f32[256]{0:T(256)S(1)} %get-tuple-element.32), channel_id=1, replica_groups=mesh['seq'=64,'dp'=8] {'seq','dp'}, use_global_device_ids=true, to_apply=%region_8.9 | all-reduce | flops 512 | bytes 4096 | tf_op jit(solution)/shard_map/psum | solution.py:115
  (68 shorter events, 2.1 us)
Async XLA Ops:
  0.6 18.4 %copy-start.9 = (bf16[1,256,512]{2,1,0:T(8,128)(2,1)S(1)}, bf16[1,256,512]{2,1,0:T(8,128)(2,1)}, u32[]{:S(2)}) copy-start(bf16[1,256,512]{2,1,0:T(8,128)(2,1)} %param.8) | copy-start | bytes 786436
  0.7 23.5 %copy-start.7 = (bf16[1,256,1024]{2,1,0:T(8,128)(2,1)S(1)}, bf16[1,256,1024]{2,1,0:T(8,128)(2,1)}, u32[]{:S(2)}) copy-start(bf16[1,256,1024]{2,1,0:T(8,128)(2,1)} %param.6) | copy-start | bytes 1572868
  3.2 22.0 %copy-start.12 = (f32[256]{0:T(256)S(1)}, f32[256]{0:T(256)}, u32[]{:S(2)}) copy-start(f32[256]{0:T(256)} %param.10) | copy-start | bytes 3076
  3.4 26.9 %collective-permute-start = (bf16[256,512]{0,1:T(8,128)(2,1)S(1)}, bf16[256,512]{0,1:T(8,128)(2,1)}, u32[]{:S(2)}, u32[]{:S(2)}) collective-permute-start(bf16[256,512]{0,1:T(8,128)(2,1)S(1)} %bitcast.80), channel_id=1, source_target_pairs={{0,32},{8,40},{16,48},{24,56},{32,64},{40,72},{48,80},{56,88},{64,... | collective-permute-start | bytes 786440 | tf_op jit(solution)/shard_map/ppermute | solution.py:15
  9.7 24.9 %collective-permute-start.1 = (bf16[256,512]{0,1:T(8,128)(2,1)S(1)}, bf16[256,512]{0,1:T(8,128)(2,1)}, u32[]{:S(2)}, u32[]{:S(2)}) collective-permute-start(bf16[256,512]{0,1:T(8,128)(2,1)S(1)} %bitcast.81), channel_id=1, source_target_pairs={{0,24},{8,32},{16,40},{24,48},{32,56},{40,64},{48,72},{56,80},{64,... | collective-permute-start | bytes 786440 | tf_op jit(solution)/shard_map/ppermute | solution.py:15
  13.9 25.6 %collective-permute-start.2 = (bf16[256,512]{0,1:T(8,128)(2,1)S(1)}, bf16[256,512]{0,1:T(8,128)(2,1)}, u32[]{:S(2)}, u32[]{:S(2)}) collective-permute-start(bf16[256,512]{0,1:T(8,128)(2,1)S(1)} %bitcast.82), channel_id=1, source_target_pairs={{0,16},{8,24},{16,32},{24,40},{32,48},{40,56},{48,64},{56,72},{64,... | collective-permute-start | bytes 786440 | tf_op jit(solution)/shard_map/ppermute | solution.py:15
  17.1 25.6 %collective-permute-start.3 = (bf16[256,512]{0,1:T(8,128)(2,1)S(1)}, bf16[256,512]{0,1:T(8,128)(2,1)}, u32[]{:S(2)}, u32[]{:S(2)}) collective-permute-start(bf16[256,512]{0,1:T(8,128)(2,1)S(1)} %bitcast.83), channel_id=1, source_target_pairs={{0,8},{8,16},{16,24},{24,32},{32,40},{40,48},{48,56},{56,64},{64,7... | collective-permute-start | bytes 786440 | tf_op jit(solution)/shard_map/ppermute | solution.py:15
  19.2 24.5 %collective-permute-start.4 = (bf16[256,512]{0,1:T(8,128)(2,1)S(1)}, bf16[256,512]{0,1:T(8,128)(2,1)}, u32[]{:S(2)}, u32[]{:S(2)}) collective-permute-start(bf16[256,512]{0,1:T(8,128)(2,1)S(1)} %bitcast.85), channel_id=1, source_target_pairs={{0,32},{8,40},{16,48},{24,56},{32,64},{40,72},{48,80},{56,88},{64,... | collective-permute-start | bytes 786440 | tf_op jit(solution)/shard_map/ppermute | solution.py:15
  24.0 2.7 %copy-start.2 = (f32[256,128]{1,0:T(8,128)}, f32[256,128]{1,0:T(8,128)S(1)}, u32[]{:S(2)}) copy-start(f32[256,128]{1,0:T(8,128)S(1)} %copy.105) | copy-start | bytes 393220
  24.1 2.6 %copy-start.3 = (f32[256,128]{1,0:T(8,128)}, f32[256,128]{1,0:T(8,128)S(1)}, u32[]{:S(2)}) copy-start(f32[256,128]{1,0:T(8,128)S(1)} %copy.104) | copy-start | bytes 393220
  30.3 15.6 %collective-permute-start.5 = (bf16[256,512]{0,1:T(8,128)(2,1)S(1)}, bf16[256,512]{0,1:T(8,128)(2,1)S(1)}, u32[]{:S(2)}, u32[]{:S(2)}) collective-permute-start(bf16[256,512]{0,1:T(8,128)(2,1)S(1)} %bitcast.87), channel_id=1, source_target_pairs={{0,24},{8,32},{16,40},{24,48},{32,56},{40,64},{48,72},{56,80},{64,... | collective-permute-start | bytes 786440 | tf_op jit(solution)/shard_map/ppermute | solution.py:15
  34.6 13.0 %collective-permute-start.6 = (bf16[256,512]{0,1:T(8,128)(2,1)S(1)}, bf16[256,512]{0,1:T(8,128)(2,1)}, u32[]{:S(2)}, u32[]{:S(2)}) collective-permute-start(bf16[256,512]{0,1:T(8,128)(2,1)S(1)} %bitcast.88), channel_id=1, source_target_pairs={{0,16},{8,24},{16,32},{24,40},{32,48},{40,56},{48,64},{56,72},{64,... | collective-permute-start | bytes 786440 | tf_op jit(solution)/shard_map/ppermute | solution.py:15
  39.5 11.4 %collective-permute-start.7 = (bf16[256,512]{0,1:T(8,128)(2,1)S(1)}, bf16[256,512]{0,1:T(8,128)(2,1)}, u32[]{:S(2)}, u32[]{:S(2)}) collective-permute-start(bf16[256,512]{0,1:T(8,128)(2,1)S(1)} %bitcast.89), channel_id=1, source_target_pairs={{0,8},{8,16},{16,24},{24,32},{32,40},{40,48},{48,56},{56,64},{64,7... | collective-permute-start | bytes 786440 | tf_op jit(solution)/shard_map/ppermute | solution.py:15
  43.6 1.1 copy-start.11
  45.8 0.7 copy-start.10
  55.0 2.4 copy-start
  55.0 2.4 copy-start.1
  55.0 2.5 copy-start.6
  55.0 2.8 %copy-start.5 = (bf16[256,2,256]{2,0,1:T(8,128)(2,1)S(1)}, bf16[256,2,256]{2,0,1:T(8,128)(2,1)}, u32[]{:S(2)}) copy-start(bf16[256,2,256]{2,0,1:T(8,128)(2,1)} %copy.114) | copy-start | bytes 786436
  61.0 10.9 %copy-start.8 = (bf16[256,4,256]{2,0,1:T(8,128)(2,1)S(1)}, bf16[256,4,256]{2,0,1:T(8,128)(2,1)}, u32[]{:S(2)}) copy-start(bf16[256,4,256]{2,0,1:T(8,128)(2,1)} %copy.106) | copy-start | bytes 1572868
  83.5 5.4 %copy-start.4 = (f32[2,256,2,256]{3,1,2,0:T(8,128)S(1)}, f32[2,256,2,256]{3,1,2,0:T(8,128)}, u32[]{:S(2)}) copy-start(f32[2,256,2,256]{3,1,2,0:T(8,128)} %fusion.6) | copy-start | bytes 3145732
  89.0 2.7 %copy-start.13 = (f32[256]{0:T(256)S(1)}, f32[256]{0:T(256)}, u32[]{:S(2)}) copy-start(f32[256]{0:T(256)} %param.10) | copy-start | bytes 3076
  96.0 13.1 %collective-permute-start.11 = (bf16[256,2,256]{0,2,1:T(8,128)(2,1)}, bf16[256,2,256]{0,2,1:T(8,128)(2,1)}, u32[]{:S(2)}, u32[]{:S(2)}) collective-permute-start(bf16[256,2,256]{0,2,1:T(8,128)(2,1)} %get-tuple-element.41), channel_id=1, source_target_pairs={{32,0},{40,8},{48,16},{56,24},{64,32},{72,40},{80,48},{88,56},{96,... | collective-permute-start | bytes 786440 | tf_op jit(solution)/shard_map/ppermute | solution.py:15
  97.3 13.3 %collective-permute-start.10 = (bf16[256,2,256]{0,2,1:T(8,128)(2,1)}, bf16[256,2,256]{0,2,1:T(8,128)(2,1)}, u32[]{:S(2)}, u32[]{:S(2)}) collective-permute-start(bf16[256,2,256]{0,2,1:T(8,128)(2,1)} %get-tuple-element.42), channel_id=1, source_target_pairs={{24,0},{32,8},{40,16},{48,24},{56,32},{64,40},{72,48},{80,56},{88,... | collective-permute-start | bytes 786440 | tf_op jit(solution)/shard_map/ppermute | solution.py:15
  98.6 23.5 %collective-permute-start.9 = (bf16[256,2,256]{0,2,1:T(8,128)(2,1)}, bf16[256,2,256]{0,2,1:T(8,128)(2,1)}, u32[]{:S(2)}, u32[]{:S(2)}) collective-permute-start(bf16[256,2,256]{0,2,1:T(8,128)(2,1)} %get-tuple-element.43), channel_id=1, source_target_pairs={{16,0},{24,8},{32,16},{40,24},{48,32},{56,40},{64,48},{72,56},{80,... | collective-permute-start | bytes 786440 | tf_op jit(solution)/shard_map/ppermute | solution.py:15
  99.9 31.0 %collective-permute-start.8 = (bf16[256,2,256]{0,2,1:T(8,128)(2,1)}, bf16[256,2,256]{0,2,1:T(8,128)(2,1)}, u32[]{:S(2)}, u32[]{:S(2)}) collective-permute-start(bf16[256,2,256]{0,2,1:T(8,128)(2,1)} %get-tuple-element.40), channel_id=1, source_target_pairs={{8,0},{16,8},{24,16},{32,24},{40,32},{48,40},{56,48},{64,56},{72,6... | collective-permute-start | bytes 786440 | tf_op jit(solution)/shard_map/ppermute | solution.py:15
  105.7 26.8 %copy-start.14 = (f32[256]{0:T(256)S(1)}, f32[256]{0:T(256)}, u32[]{:S(2)}) copy-start(f32[256]{0:T(256)} %param.11) | copy-start | bytes 3076
  107.8 25.9 %collective-permute-start.15 = (bf16[256,2,256]{0,2,1:T(8,128)(2,1)}, bf16[256,2,256]{0,2,1:T(8,128)(2,1)S(1)}, u32[]{:S(2)}, u32[]{:S(2)}) collective-permute-start(bf16[256,2,256]{0,2,1:T(8,128)(2,1)} %get-tuple-element.37), channel_id=1, source_target_pairs={{32,0},{40,8},{48,16},{56,24},{64,32},{72,40},{80,48},{88,56},{96,... | collective-permute-start | bytes 786440 | tf_op jit(solution)/shard_map/ppermute | solution.py:15
  109.1 24.6 %collective-permute-start.14 = (bf16[256,2,256]{0,2,1:T(8,128)(2,1)}, bf16[256,2,256]{0,2,1:T(8,128)(2,1)S(1)}, u32[]{:S(2)}, u32[]{:S(2)}) collective-permute-start(bf16[256,2,256]{0,2,1:T(8,128)(2,1)} %get-tuple-element.38), channel_id=1, source_target_pairs={{24,0},{32,8},{40,16},{48,24},{56,32},{64,40},{72,48},{80,56},{88,... | collective-permute-start | bytes 786440 | tf_op jit(solution)/shard_map/ppermute | solution.py:15
  110.6 29.5 %collective-permute-start.13 = (bf16[256,2,256]{0,2,1:T(8,128)(2,1)S(1)}, bf16[256,2,256]{0,2,1:T(8,128)(2,1)S(1)}, u32[]{:S(2)}, u32[]{:S(2)}) collective-permute-start(bf16[256,2,256]{0,2,1:T(8,128)(2,1)S(1)} %get-tuple-element.39), channel_id=1, source_target_pairs={{16,0},{24,8},{32,16},{40,24},{48,32},{56,40},{64,48},{72,56},{80,... | collective-permute-start | bytes 786440 | tf_op jit(solution)/shard_map/ppermute | solution.py:15
  122.1 19.9 %collective-permute-start.12 = (bf16[256,2,256]{0,2,1:T(8,128)(2,1)S(1)}, bf16[256,2,256]{0,2,1:T(8,128)(2,1)S(1)}, u32[]{:S(2)}, u32[]{:S(2)}) collective-permute-start(bf16[256,2,256]{0,2,1:T(8,128)(2,1)S(1)} %get-tuple-element.36), channel_id=1, source_target_pairs={{8,0},{16,8},{24,16},{32,24},{40,32},{48,40},{56,48},{64,56},{72,6... | collective-permute-start | bytes 786440 | tf_op jit(solution)/shard_map/ppermute | solution.py:15
  132.5 11.5 %copy-start.15 = (f32[256]{0:T(256)S(1)}, f32[256]{0:T(256)}, u32[]{:S(2)}) copy-start(f32[256]{0:T(256)} %get-tuple-element.30) | copy-start | bytes 3076
where the time goes:
time: 259 us; the launch traced here: 258 us
  blocking collectives  114 us (44%)
  starting transfers between devices  42.5 us (16%)
  matrix products  34.2 us (13%)
  local copies, waits for them, and re-layouts  28.6 us (11%)
  waiting for transfers between devices  25.6 us (10%)
  other arithmetic  11.9 us (5%)
    psum x1, blocking collectives, local(): lax.psum((gain_q_local, gain_k_local), ('seq', 'dp'))  114 us
    ppermute x16, starting transfers between devices, from_behind(): return lax.ppermute(array, axis, pairs)  42.5 us
    ppermute x16, waiting for transfers between devices, from_behind(): return lax.ppermute(array, axis, pairs)  25.6 us
    dot_general x1, matrix products, local(): jnp.einsum('kgts,tkgd->skd', dscores, q_heads, preferred_element_type=jnp...  11.7 us
    unnamed x45, local copies, waits for them, and re-layouts  11.5 us
    dot_general x1, matrix products, local(): jnp.einsum('kgts,skd->tkgd', dscores, k_heads, preferred_element_type=jnp...  10.9 us
    concatenate x6, local copies, waits for them, and re-layouts, local(): value_rows = jnp.concatenate(halo_v + [v_local], axis=0)  5.89 us
    dot_general x1, matrix products, local(): jnp.einsum('kgts,tkgd->skd', weights_b, do_heads, preferred_element_type=...  5.41 us
  transfers between devices with their start and end apart: 16, of which 5 were waited for; matrix products, arithmetic and copies ran while one was open for 9% of the time, Pallas kernels for 0%

commit v1 on v0

--- a/solution.py
+++ b/solution.py
@@ -112,7 +112,7 @@
     dk_rot = dk_own.reshape(rows_here, pair_heads * head_size)
     grad_q_local, gain_q_local = q_back(dq_rot)
     grad_k_local, gain_k_local = k_back(dk_rot)
-    gain_q_all, gain_k_all = lax.psum((gain_q_local, gain_k_local), ("seq", "dp"))
+    gain_q_all, gain_k_all = lax.psum(lax.psum((gain_q_local, gain_k_local), "dp"), "seq")
     grad_v_local = dv_own.reshape(rows_here, pair_heads * head_size).astype(jnp.bfloat16)
     return (
         grad_q_local.astype(jnp.bfloat16)[None],

time: 259 us -> 400 us (1.54)
  blocking collectives: 114 us -> 255 us
    psum x1 -> x2, blocking collectives: 114 us -> 255 us  [the longest x1 211 us: local(): lax.psum(lax.psum((gain_q_local, gain_k_local), 'dp'), 'seq')]
  transfers between devices with their start and end apart: 16 -> 16, of which waited for: 5 -> 5; matrix products, arithmetic and copies ran while one was open for 9% -> 6% of each run, Pallas kernels for 0% -> 0%
where the time goes in v1:
time: 400 us; the launch traced here: 399 us
  blocking collectives  255 us (64%)
  starting transfers between devices  42.5 us (11%)
  matrix products  34.2 us (9%)
  local copies, waits for them, and re-layouts  27.8 us (7%)
  waiting for transfers between devices  26.4 us (7%)
  other arithmetic  11.9 us (3%)
    psum x1, blocking collectives, local(): lax.psum(lax.psum((gain_q_local, gain_k_local), 'dp'), 'seq')  211 us
    psum x1, blocking collectives, local(): lax.psum((gain_q_local, gain_k_local), 'dp')  43.8 us
    ppermute x16, starting transfers between devices, from_behind(): return lax.ppermute(array, axis, pairs)  42.5 us
    ppermute x16, waiting for transfers between devices, from_behind(): return lax.ppermute(array, axis, pairs)  26.4 us
    dot_general x1, matrix products, local(): jnp.einsum('kgts,tkgd->skd', dscores, q_heads, preferred_element_type=jnp...  11.7 us
    unnamed x45, local copies, waits for them, and re-layouts  11.5 us
    dot_general x1, matrix products, local(): jnp.einsum('kgts,skd->tkgd', dscores, k_heads, preferred_element_type=jnp...  10.9 us
  transfers between devices with their start and end apart: 16, of which 5 were waited for; matrix products, arithmetic and copies ran while one was open for 6% of the time, Pallas kernels for 0%

profile of v1, /device:TPU:1, one launch (start us, length us, event | category | flops | bytes accessed | tf_op | source)
XLA Modules:
  0.0 399.2 jit_solution(9458186133957766319)
XLA Ops:
  0.7 1.1 copy.101
  1.9 0.8 multiply_multiply_fusion.1
  2.7 0.5 multiply_cosine_fusion
  3.4 6.4 %collective-permute-start = (bf16[256,512]{0,1:T(8,128)(2,1)S(1)}, bf16[256,512]{0,1:T(8,128)(2,1)}, u32[]{:S(2)}, u32[]{:S(2)}) collective-permute-start(bf16[256,512]{0,1:T(8,128)(2,1)S(1)} %bitcast.80), channel_id=1, source_target_pairs={{0,32},{8,40},{16,48},{24,56},{32,64},{40,72},{48,80},{56,88},{64,... | collective-permute-start | bytes 786440 | tf_op jit(solution)/shard_map/ppermute | solution.py:15
  9.7 4.2 %collective-permute-start.1 = (bf16[256,512]{0,1:T(8,128)(2,1)S(1)}, bf16[256,512]{0,1:T(8,128)(2,1)}, u32[]{:S(2)}, u32[]{:S(2)}) collective-permute-start(bf16[256,512]{0,1:T(8,128)(2,1)S(1)} %bitcast.81), channel_id=1, source_target_pairs={{0,24},{8,32},{16,40},{24,48},{32,56},{40,64},{48,72},{56,80},{64,... | collective-permute-start | bytes 786440 | tf_op jit(solution)/shard_map/ppermute | solution.py:15
  13.9 3.2 collective-permute-start.2
  17.1 1.9 collective-permute-start.3
  19.2 4.7 %collective-permute-start.4 = (bf16[256,512]{0,1:T(8,128)(2,1)S(1)}, bf16[256,512]{0,1:T(8,128)(2,1)}, u32[]{:S(2)}, u32[]{:S(2)}) collective-permute-start(bf16[256,512]{0,1:T(8,128)(2,1)S(1)} %bitcast.85), channel_id=1, source_target_pairs={{0,32},{8,40},{16,48},{24,56},{32,64},{40,72},{48,80},{56,88},{64,... | collective-permute-start | bytes 786440 | tf_op jit(solution)/shard_map/ppermute | solution.py:15
  24.1 0.5 reshape.191
  24.6 0.3 multiply_reduce_fusion.2
  25.2 0.3 multiply_multiply_fusion
  25.6 1.1 fusion.20
  27.3 1.2 copy.142
  28.5 0.8 copy.114
  29.4 0.9 copy.106
  30.2 3.4 collective-permute-start.5
  33.6 1.0 constant_dynamic-update-slice_fusion.4
  34.6 3.9 collective-permute-start.6
  38.5 1.0 constant_dynamic-update-slice_fusion.3
  39.5 2.2 collective-permute-start.7
  41.7 1.0 constant_dynamic-update-slice_fusion.2
  42.7 1.0 constant_dynamic-update-slice_fusion.1
  43.7 1.1 copy-done.11
  44.7 1.1 copy.110
  45.8 0.7 copy-done.10
  46.5 1.1 copy.111
  47.6 1.8 copy.112
  49.4 0.7 constant_dynamic-update-slice_fusion
  50.1 0.7 constant_dynamic-update-slice_fusion.9
  50.9 1.1 copy.113
  52.0 3.0 fusion.39
  55.0 0.7 exponential_reduce_fusion
  55.7 1.7 copy-done
  57.8 3.2 fusion.15
  61.0 10.9 %fusion.6 = f32[2,256,2,256]{3,1,2,0:T(8,128)} fusion(bf16[1280,2,256,1]{0,2,3,1:T(8,128)(2,1)} %bitcast.95, f32[2,1280,256,2]{2,1,3,0:T(8,128)} %fusion.15, f32[2,2,256,1280]{2,3,1,0:T(8,128)} %copy-done, f32[2,2,256]{2,1,0:T(2,128)S(1)} %log_add_fusion), kind=kOutput, calls=%fused_computation.13 | convolution fusion | flops 680265984 | bytes 12849152 | tf_op jit(solution)/shard_map/kgts,skd->tkgd/dot_general | solution.py:98
  71.8 11.7 %fusion.40 = (bf16[1280,2,256]{0,2,1:T(8,128)(2,1)}, f32[1280,2,256]{0,2,1:T(8,128)}) fusion(bf16[256,2,2,256]{3,0,2,1:T(8,128)(2,1)S(1)} %bitcast.92, f32[2,1280,256,2]{2,1,3,0:T(8,128)} %fusion.15, f32[2,2,256,1280]{2,3,1,0:T(8,128)} %copy-done, f32[2,2,256]{2,1,0:T(2,128)S(1)} %log_add_fusion), kind=kOutput, calls=%fused_computation.90 | convolution fusion | flops 680921344 | bytes 14946304 | tf_op jit(solution)/shard_map/kgts,tkgd->skd/dot_general | solution.py:101
  83.6 5.4 %fusion.41 = (bf16[1280,2,256]{0,2,1:T(8,128)(2,1)}, f32[1280,2,256]{0,2,1:T(8,128)}) fusion(bf16[256,2,2,256]{0,3,2,1:T(8,128)(2,1)S(1)} %bitcast.77, f32[2,2,256,1280]{2,3,1,0:T(8,128)} %copy-done, f32[2,2,256]{2,1,0:T(2,128)S(1)} %log_add_fusion), kind=kOutput, calls=%fused_computation.91 | convolution fusion | flops 674365440 | bytes 9703424 | tf_op jit(solution)/shard_map/kgts,tkgd->skd/dot_general | solution.py:102
  89.3 1.0 copy.140
  90.3 1.4 multiply_add_fusion.1
  91.7 1.2 multiply_reduce_fusion
  93.0 0.8 copy.120
  93.9 2.2 fusion.37
  96.0 1.3 collective-permute-start.11
  97.3 1.3 collective-permute-start.10
  98.6 1.3 collective-permute-start.9
  99.9 3.1 collective-permute-start.8
  103.0 1.6 fusion.21
  104.6 1.2 convert_element_type.124
  105.7 1.3 fusion.36
  107.0 1.3 collective-permute-start.15
  108.3 1.3 collective-permute-start.14
  109.6 1.0 collective-permute-done.10
  110.6 1.3 collective-permute-start.13
  111.9 11.5 %collective-permute-done.9 = bf16[256,2,256]{0,2,1:T(8,128)(2,1)} collective-permute-done((bf16[256,2,256]{0,2,1:T(8,128)(2,1)}, bf16[256,2,256]{0,2,1:T(8,128)(2,1)}, u32[]{:S(2)}, u32[]{:S(2)}) %collective-permute-start.9) | collective-permute-done | bytes 262176 | tf_op jit(solution)/shard_map/ppermute | solution.py:15
  123.3 1.9 collective-permute-start.12
  125.2 6.9 %collective-permute-done.8 = bf16[256,2,256]{0,2,1:T(8,128)(2,1)} collective-permute-done((bf16[256,2,256]{0,2,1:T(8,128)(2,1)}, bf16[256,2,256]{0,2,1:T(8,128)(2,1)}, u32[]{:S(2)}, u32[]{:S(2)}) %collective-permute-start.8) | collective-permute-done | bytes 262176 | tf_op jit(solution)/shard_map/ppermute | solution.py:15
  132.2 1.5 fusion.29
  134.1 0.8 copy.125
  135.0 5.1 %collective-permute-done.13 = bf16[256,2,256]{0,2,1:T(8,128)(2,1)S(1)} collective-permute-done((bf16[256,2,256]{0,2,1:T(8,128)(2,1)S(1)}, bf16[256,2,256]{0,2,1:T(8,128)(2,1)S(1)}, u32[]{:S(2)}, u32[]{:S(2)}) %collective-permute-start.13) | collective-permute-done | bytes 262176 | tf_op jit(solution)/shard_map/ppermute | solution.py:15
  140.0 1.9 collective-permute-done.12
  142.0 1.2 fusion.26
  143.2 0.8 copy.126
  144.0 43.8 %all-reduce.5 = (f32[256]{0:T(256)S(1)}, f32[256]{0:T(256)S(1)}) all-reduce(f32[256]{0:T(256)S(1)} %copy-done.15, f32[256]{0:T(256)S(1)} %get-tuple-element.32), channel_id=1, replica_groups=mesh['seq'=64,'dp'=8] {'dp'}, use_global_device_ids=true, to_apply=%region_8.9 | all-reduce | flops 512 | bytes 4096 | tf_op jit(solution)/shard_map/psum | solution.py:115
  187.9 211.3 %all-reduce.4 = (f32[256]{0:T(256)}, f32[256]{0:T(256)}) all-reduce(f32[256]{0:T(256)S(1)} %get-tuple-element.36, f32[256]{0:T(256)S(1)} %get-tuple-element.37), channel_id=1, replica_groups=mesh['seq'=64,'dp'=8] {'seq'}, use_global_device_ids=true, to_apply=%region_9.10 | all-reduce | flops 512 | bytes 4096 | tf_op jit(solution)/shard_map/psum | solution.py:115
  (69 shorter events, 2.6 us)
Async XLA Ops:
  0.6 18.4 %copy-start.9 = (bf16[1,256,512]{2,1,0:T(8,128)(2,1)S(1)}, bf16[1,256,512]{2,1,0:T(8,128)(2,1)}, u32[]{:S(2)}) copy-start(bf16[1,256,512]{2,1,0:T(8,128)(2,1)} %param.8) | copy-start | bytes 786436
  0.7 23.5 %copy-start.7 = (bf16[1,256,1024]{2,1,0:T(8,128)(2,1)S(1)}, bf16[1,256,1024]{2,1,0:T(8,128)(2,1)}, u32[]{:S(2)}) copy-start(bf16[1,256,1024]{2,1,0:T(8,128)(2,1)} %param.6) | copy-start | bytes 1572868
  3.2 22.0 %copy-start.12 = (f32[256]{0:T(256)S(1)}, f32[256]{0:T(256)}, u32[]{:S(2)}) copy-start(f32[256]{0:T(256)} %param.10) | copy-start | bytes 3076
  3.4 26.9 %collective-permute-start = (bf16[256,512]{0,1:T(8,128)(2,1)S(1)}, bf16[256,512]{0,1:T(8,128)(2,1)}, u32[]{:S(2)}, u32[]{:S(2)}) collective-permute-start(bf16[256,512]{0,1:T(8,128)(2,1)S(1)} %bitcast.80), channel_id=1, source_target_pairs={{0,32},{8,40},{16,48},{24,56},{32,64},{40,72},{48,80},{56,88},{64,... | collective-permute-start | bytes 786440 | tf_op jit(solution)/shard_map/ppermute | solution.py:15
  9.7 24.9 %collective-permute-start.1 = (bf16[256,512]{0,1:T(8,128)(2,1)S(1)}, bf16[256,512]{0,1:T(8,128)(2,1)}, u32[]{:S(2)}, u32[]{:S(2)}) collective-permute-start(bf16[256,512]{0,1:T(8,128)(2,1)S(1)} %bitcast.81), channel_id=1, source_target_pairs={{0,24},{8,32},{16,40},{24,48},{32,56},{40,64},{48,72},{56,80},{64,... | collective-permute-start | bytes 786440 | tf_op jit(solution)/shard_map/ppermute | solution.py:15
  13.9 25.6 %collective-permute-start.2 = (bf16[256,512]{0,1:T(8,128)(2,1)S(1)}, bf16[256,512]{0,1:T(8,128)(2,1)}, u32[]{:S(2)}, u32[]{:S(2)}) collective-permute-start(bf16[256,512]{0,1:T(8,128)(2,1)S(1)} %bitcast.82), channel_id=1, source_target_pairs={{0,16},{8,24},{16,32},{24,40},{32,48},{40,56},{48,64},{56,72},{64,... | collective-permute-start | bytes 786440 | tf_op jit(solution)/shard_map/ppermute | solution.py:15
  17.1 25.5 %collective-permute-start.3 = (bf16[256,512]{0,1:T(8,128)(2,1)S(1)}, bf16[256,512]{0,1:T(8,128)(2,1)}, u32[]{:S(2)}, u32[]{:S(2)}) collective-permute-start(bf16[256,512]{0,1:T(8,128)(2,1)S(1)} %bitcast.83), channel_id=1, source_target_pairs={{0,8},{8,16},{16,24},{24,32},{32,40},{40,48},{48,56},{56,64},{64,7... | collective-permute-start | bytes 786440 | tf_op jit(solution)/shard_map/ppermute | solution.py:15
  19.2 24.5 %collective-permute-start.4 = (bf16[256,512]{0,1:T(8,128)(2,1)S(1)}, bf16[256,512]{0,1:T(8,128)(2,1)}, u32[]{:S(2)}, u32[]{:S(2)}) collective-permute-start(bf16[256,512]{0,1:T(8,128)(2,1)S(1)} %bitcast.85), channel_id=1, source_target_pairs={{0,32},{8,40},{16,48},{24,56},{32,64},{40,72},{48,80},{56,88},{64,... | collective-permute-start | bytes 786440 | tf_op jit(solution)/shard_map/ppermute | solution.py:15
  24.0 2.7 copy-start.2
  24.1 2.6 copy-start.3
  30.2 15.6 %collective-permute-start.5 = (bf16[256,512]{0,1:T(8,128)(2,1)S(1)}, bf16[256,512]{0,1:T(8,128)(2,1)S(1)}, u32[]{:S(2)}, u32[]{:S(2)}) collective-permute-start(bf16[256,512]{0,1:T(8,128)(2,1)S(1)} %bitcast.87), channel_id=1, source_target_pairs={{0,24},{8,32},{16,40},{24,48},{32,56},{40,64},{48,72},{56,80},{64,... | collective-permute-start | bytes 786440 | tf_op jit(solution)/shard_map/ppermute | solution.py:15
  34.6 13.0 %collective-permute-start.6 = (bf16[256,512]{0,1:T(8,128)(2,1)S(1)}, bf16[256,512]{0,1:T(8,128)(2,1)}, u32[]{:S(2)}, u32[]{:S(2)}) collective-permute-start(bf16[256,512]{0,1:T(8,128)(2,1)S(1)} %bitcast.88), channel_id=1, source_target_pairs={{0,16},{8,24},{16,32},{24,40},{32,48},{40,56},{48,64},{56,72},{64,... | collective-permute-start | bytes 786440 | tf_op jit(solution)/shard_map/ppermute | solution.py:15
  39.5 11.4 %collective-permute-start.7 = (bf16[256,512]{0,1:T(8,128)(2,1)S(1)}, bf16[256,512]{0,1:T(8,128)(2,1)}, u32[]{:S(2)}, u32[]{:S(2)}) collective-permute-start(bf16[256,512]{0,1:T(8,128)(2,1)S(1)} %bitcast.89), channel_id=1, source_target_pairs={{0,8},{8,16},{16,24},{24,32},{32,40},{40,48},{48,56},{56,64},{64,7... | collective-permute-start | bytes 786440 | tf_op jit(solution)/shard_map/ppermute | solution.py:15
  43.6 1.1 copy-start.11
  45.8 0.7 copy-start.10
  55.0 2.4 copy-start
  55.0 2.4 copy-start.1
  55.0 2.5 copy-start.6
  55.0 2.8 copy-start.5
  61.0 10.9 %copy-start.8 = (bf16[256,4,256]{2,0,1:T(8,128)(2,1)S(1)}, bf16[256,4,256]{2,0,1:T(8,128)(2,1)}, u32[]{:S(2)}) copy-start(bf16[256,4,256]{2,0,1:T(8,128)(2,1)} %copy.106) | copy-start | bytes 1572868
  83.6 5.4 %copy-start.4 = (f32[2,256,2,256]{3,1,2,0:T(8,128)S(1)}, f32[2,256,2,256]{3,1,2,0:T(8,128)}, u32[]{:S(2)}) copy-start(f32[2,256,2,256]{3,1,2,0:T(8,128)} %fusion.6) | copy-start | bytes 3145732
  89.0 2.7 copy-start.13
  96.0 12.3 %collective-permute-start.11 = (bf16[256,2,256]{0,2,1:T(8,128)(2,1)}, bf16[256,2,256]{0,2,1:T(8,128)(2,1)}, u32[]{:S(2)}, u32[]{:S(2)}) collective-permute-start(bf16[256,2,256]{0,2,1:T(8,128)(2,1)} %get-tuple-element.43), channel_id=1, source_target_pairs={{32,0},{40,8},{48,16},{56,24},{64,32},{72,40},{80,48},{88,56},{96,... | collective-permute-start | bytes 786440 | tf_op jit(solution)/shard_map/ppermute | solution.py:15
  97.3 13.3 %collective-permute-start.10 = (bf16[256,2,256]{0,2,1:T(8,128)(2,1)}, bf16[256,2,256]{0,2,1:T(8,128)(2,1)}, u32[]{:S(2)}, u32[]{:S(2)}) collective-permute-start(bf16[256,2,256]{0,2,1:T(8,128)(2,1)} %get-tuple-element.44), channel_id=1, source_target_pairs={{24,0},{32,8},{40,16},{48,24},{56,32},{64,40},{72,48},{80,56},{88,... | collective-permute-start | bytes 786440 | tf_op jit(solution)/shard_map/ppermute | solution.py:15
  98.6 24.7 %collective-permute-start.9 = (bf16[256,2,256]{0,2,1:T(8,128)(2,1)}, bf16[256,2,256]{0,2,1:T(8,128)(2,1)}, u32[]{:S(2)}, u32[]{:S(2)}) collective-permute-start(bf16[256,2,256]{0,2,1:T(8,128)(2,1)} %get-tuple-element.45), channel_id=1, source_target_pairs={{16,0},{24,8},{32,16},{40,24},{48,32},{56,40},{64,48},{72,56},{80,... | collective-permute-start | bytes 786440 | tf_op jit(solution)/shard_map/ppermute | solution.py:15
  99.9 32.3 %collective-permute-start.8 = (bf16[256,2,256]{0,2,1:T(8,128)(2,1)}, bf16[256,2,256]{0,2,1:T(8,128)(2,1)}, u32[]{:S(2)}, u32[]{:S(2)}) collective-permute-start(bf16[256,2,256]{0,2,1:T(8,128)(2,1)} %get-tuple-element.42), channel_id=1, source_target_pairs={{8,0},{16,8},{24,16},{32,24},{40,32},{48,40},{56,48},{64,56},{72,6... | collective-permute-start | bytes 786440 | tf_op jit(solution)/shard_map/ppermute | solution.py:15
  105.7 28.0 %copy-start.14 = (f32[256]{0:T(256)S(1)}, f32[256]{0:T(256)}, u32[]{:S(2)}) copy-start(f32[256]{0:T(256)} %param.11) | copy-start | bytes 3076
  107.0 28.0 %collective-permute-start.15 = (bf16[256,2,256]{0,2,1:T(8,128)(2,1)S(1)}, bf16[256,2,256]{0,2,1:T(8,128)(2,1)S(1)}, u32[]{:S(2)}, u32[]{:S(2)}) collective-permute-start(bf16[256,2,256]{0,2,1:T(8,128)(2,1)S(1)} %get-tuple-element.39), channel_id=1, source_target_pairs={{32,0},{40,8},{48,16},{56,24},{64,32},{72,40},{80,48},{88,56},{96,... | collective-permute-start | bytes 786440 | tf_op jit(solution)/shard_map/ppermute | solution.py:15
  108.3 26.7 %collective-permute-start.14 = (bf16[256,2,256]{0,2,1:T(8,128)(2,1)S(1)}, bf16[256,2,256]{0,2,1:T(8,128)(2,1)S(1)}, u32[]{:S(2)}, u32[]{:S(2)}) collective-permute-start(bf16[256,2,256]{0,2,1:T(8,128)(2,1)S(1)} %get-tuple-element.40), channel_id=1, source_target_pairs={{24,0},{32,8},{40,16},{48,24},{56,32},{64,40},{72,48},{80,56},{88,... | collective-permute-start | bytes 786440 | tf_op jit(solution)/shard_map/ppermute | solution.py:15
  110.6 29.5 %collective-permute-start.13 = (bf16[256,2,256]{0,2,1:T(8,128)(2,1)S(1)}, bf16[256,2,256]{0,2,1:T(8,128)(2,1)S(1)}, u32[]{:S(2)}, u32[]{:S(2)}) collective-permute-start(bf16[256,2,256]{0,2,1:T(8,128)(2,1)S(1)} %get-tuple-element.41), channel_id=1, source_target_pairs={{16,0},{24,8},{32,16},{40,24},{48,32},{56,40},{64,48},{72,56},{80,... | collective-permute-start | bytes 786440 | tf_op jit(solution)/shard_map/ppermute | solution.py:15
  123.3 18.6 %collective-permute-start.12 = (bf16[256,2,256]{0,2,1:T(8,128)(2,1)S(1)}, bf16[256,2,256]{0,2,1:T(8,128)(2,1)S(1)}, u32[]{:S(2)}, u32[]{:S(2)}) collective-permute-start(bf16[256,2,256]{0,2,1:T(8,128)(2,1)S(1)} %get-tuple-element.38), channel_id=1, source_target_pairs={{8,0},{16,8},{24,16},{32,24},{40,32},{48,40},{56,48},{64,56},{72,6... | collective-permute-start | bytes 786440 | tf_op jit(solution)/shard_map/ppermute | solution.py:15
  133.8 10.3 %copy-start.15 = (f32[256]{0:T(256)S(1)}, f32[256]{0:T(256)}, u32[]{:S(2)}) copy-start(f32[256]{0:T(256)} %get-tuple-element.30) | copy-start | bytes 3076
